TPU v7x, 128 devices: a whole 4x4x4 slice. The times are simulated.
128 devices in a mesh: prow: 8 (over y_lo, x), pcol: 16 (over y_hi, z, core).
Axes of the slice: x: 4, y: 4 (y_hi: 2, y_lo: 2; y = y_hi * 2 + y_lo), z: 4, core: 2. Of those that a mesh axis runs over, the one named last changes fastest.
Arguments:
- l_panel: bfloat16 [16384, 2048], P('prow', 'pcol'), may hold values from -0.29882812 to 0.29882812
- inverse_tile: bfloat16 [16384, 16384], P('prow', 'pcol'), may hold values from -0.375 to 0.375
- unit_inverse: bfloat16 [16, 128, 128], P('pcol'), may hold values from -0.5 to 0.5
- pivot_inverse: float32 [16, 128, 128], P('pcol'), may hold values from -6 to 6
- listed: int32 [16, 128], replicated, may hold values 0 or 1
Outputs:
- offdiag: float32 [2048, 16384], P('pcol', 'prow')
- diag: float32 [16, 128, 128], P('pcol')
All inputs are finite; a program needn't handle non-finite values.
Results may differ from a plain program's by a relative error of at most 0.015.
Values may be sent and summed in bfloat16 or wider, within the bound.
A program may use at most 64 MiB of HBM per device.

v0:
```python
import jax
import jax.numpy as jnp
from jax import lax
from jax.sharding import PartitionSpec as P

BLOCK = 128


def broadcast(block, axis, source):
    block = jnp.where(lax.axis_index(axis) == source, block, jnp.zeros_like(block))
    return lax.psum(block, axis)


def per_device(l_panel, inverse_tile, unit_inverse, pivot_inverse, listed):
    rows = l_panel.shape[0]
    columns = inverse_tile.shape[1]
    count_sn = unit_inverse.shape[0]
    width = unit_inverse.shape[1]
    row_index = lax.axis_index("prow")
    col_index = lax.axis_index("pcol")
    blocks = rows // BLOCK
    mine = lax.dynamic_slice(listed, (col_index * count_sn, row_index * blocks), (count_sn, blocks))
    row_mask = jnp.repeat(mine, BLOCK, axis=1).astype(jnp.bfloat16)
    masked = l_panel.reshape(rows, count_sn, width) * row_mask.T[:, :, None]
    lhat = jnp.einsum(
        "nsw,swv->nsv", masked, unit_inverse, preferred_element_type=jnp.float32
    ).astype(jnp.bfloat16)
    lhat_flat = lhat.reshape(rows, count_sn * width)
    ratio = lax.axis_size("pcol") // lax.axis_size("prow")
    wide_rows = lax.all_gather(lhat_flat, "pcol", axis=1, tiled=True)
    source = broadcast(wide_rows, "prow", col_index // ratio)
    mirrored = lax.dynamic_slice_in_dim(source, col_index % ratio * columns, columns, 0)
    product_t = lax.psum_scatter(
        lax.dot_general(
            mirrored, inverse_tile, (((0,), (1,)), ((), ())), preferred_element_type=jnp.float32
        ).astype(jnp.bfloat16),
        "pcol",
        scatter_dimension=0,
        tiled=True,
    ).astype(jnp.float32)
    wide_mask = jnp.repeat(row_mask.astype(jnp.float32), width, axis=0)
    offdiag = -(product_t * wide_mask)
    stacked = product_t.reshape(count_sn, width, rows)
    partial_diag = jnp.einsum(
        "svn,nsw->svw", stacked, lhat.astype(jnp.float32), precision=lax.Precision.HIGHEST
    )
    total = lax.psum(partial_diag.astype(jnp.bfloat16), "prow").astype(jnp.float32)
    diag = pivot_inverse + total
    return (offdiag, diag)


def solution(mesh):
    return jax.shard_map(
        per_device,
        mesh=mesh,
        in_specs=(
            P("prow", "pcol"),
            P("prow", "pcol"),
            P("pcol", None, None),
            P("pcol", None, None),
            P(),
        ),
        out_specs=(P("pcol", "prow"), P("pcol", None, None)),
        check_vma=False,
    )
```

profile of v0, /device:TPU:0, one launch (start us, length us, event | category | flops | bytes accessed | tf_op | source)
XLA Modules:
  0.0 439.2 jit_solution(7294961271793885270)
XLA Ops:
  7.2 0.0 copy-start
  7.2 0.0 all-gather.2.cloned.1.call-start
  7.2 0.8 convert_bitcast_fusion
  8.0 0.1 bitcast_convert_fusion
  8.1 0.0 copy-done
  8.1 2.3 convolution_convert_fusion.1
  10.4 0.0 all-gather.2.cloned.1.call-update
  10.4 0.0 all-reduce.2.cloned.1.call-start
  10.5 80.2 %all-gather.2.cloned.1.call-done = bf16[2048,2048]{1,0:T(8,128)(2,1)} async-done(((bf16[2048,128]{1,0:T(8,128)(2,1)}), bf16[2048,2048]{1,0:T(8,128)(2,1)}) %all-gather.2.cloned.1.call-update) | async-done | bytes 8388624 | tf_op jit(solution)/shard_map/all_gather | solution.py:30
  90.6 7.1 %broadcast_select_fusion = bf16[2048,2048]{1,0:T(8,128)(2,1)} fusion(bf16[2048,2048]{1,0:T(8,128)(2,1)} %all-gather.2.cloned.1.call-done, pred[]{:T(512)S(6)} %eq.5), kind=kLoop, calls=%fused_computation | loop fusion | flops 4194304 | bytes 16777216 | tf_op jit(solution)/shard_map/jit(_where)/select_n | solution.py:10
  97.8 0.0 all-reduce.2.cloned.1.call-update
  97.8 0.0 reduce-scatter.2.cloned.1.call-start
  97.9 181.8 %all-reduce.2.cloned.1.call-done = bf16[2048,2048]{1,0:T(8,128)(2,1)} async-done(((bf16[2048,2048]{1,0:T(8,128)(2,1)}), bf16[2048,2048]{1,0:T(8,128)(2,1)}) %all-reduce.2.cloned.1.call-update) | async-done | bytes 8388624 | tf_op jit(solution)/shard_map/psum | solution.py:11
  279.6 14.0 %convolution_convert_fusion = bf16[2048,2048]{1,0:T(8,128)(2,1)} fusion(bf16[2048,1024]{1,0:T(8,128)(2,1)} %param.6, bf16[2048,2048]{1,0:T(8,128)(2,1)} %all-reduce.2.cloned.1.call-done, s32[]{:T(128)S(6)} %select_n.34), kind=kOutput, calls=%fused_computation.1 | convolution fusion | flops 8594128896 | bytes 16777220 | tf_op jit(solution)/shard_map/dot_general | solution.py:34
  293.6 0.0 copy-start.1
  293.6 0.0 copy-start.2
  293.6 0.0 reduce-scatter.2.cloned.1.call-update
  293.7 101.6 %reduce-scatter.2.cloned.1.call-done = bf16[128,2048]{1,0:T(8,128)(2,1)} async-done(((bf16[2048,2048]{1,0:T(8,128)(2,1)}), bf16[128,2048]{1,0:T(8,128)(2,1)}) %reduce-scatter.2.cloned.1.call-update) | async-done | bytes 524304 | tf_op jit(solution)/shard_map/reduce_scatter | solution.py:33
  395.2 0.0 copy-done.1
  395.2 1.3 fusion.1
  396.6 33.3 %psum.15 = bf16[1,128,128]{2,1,0:T(8,128)(2,1)S(1)} all-reduce(bf16[1,128,128]{2,1,0:T(8,128)(2,1)S(1)} %fusion.1), channel_id=1, replica_groups=mesh['prow'=8,'pcol'=16] {'prow'}, use_global_device_ids=true, to_apply=%region_2.3 | all-reduce | flops 16384 | bytes 65536 | tf_op jit(solution)/shard_map/psum | solution.py:47
  429.9 0.0 copy-done.2
  429.9 0.6 convert_add_fusion
  430.5 2.2 multiply_negate_fusion
Async XLA Ops:
  7.2 0.9 copy-start
  7.2 83.4 %all-gather.2.cloned.1.call-start = ((), (), s32[]{:S(2)}) async-start(), calls=%async_computation.1 | async-start | bytes 8912896 | tf_op jit(solution)/shard_map/all_gather | solution.py:30
  10.4 269.2 %all-reduce.2.cloned.1.call-start = ((), (), s32[]{:S(2)}) async-start(), calls=%async_computation.2 | async-start | bytes 16777216 | tf_op jit(solution)/shard_map/psum | solution.py:11
  97.8 297.4 %reduce-scatter.2.cloned.1.call-start = ((), (), s32[]{:S(2)}) async-start(), calls=%async_computation.3 | async-start | bytes 8912896 | tf_op jit(solution)/shard_map/reduce_scatter | solution.py:33
  293.6 101.6 %copy-start.1 = (bf16[2048,128]{1,0:T(8,128)(2,1)S(1)}, bf16[2048,128]{1,0:T(8,128)(2,1)}, u32[]{:S(2)}) copy-start(bf16[2048,128]{1,0:T(8,128)(2,1)} %convolution_convert_fusion.1) | copy-start | bytes 1572868
  293.6 136.2 %copy-start.2 = (f32[1,128,128]{2,1,0:T(8,128)S(1)}, f32[1,128,128]{2,1,0:T(8,128)}, u32[]{:S(2)}) copy-start(f32[1,128,128]{2,1,0:T(8,128)} %param.8) | copy-start | bytes 196612
Sparse Core Ops, SparseCore 0:
  10.9 79.7 all-gather.1
  97.9 181.6 all-reduce.1
  293.8 101.3 reduce-scatter.1
where the time goes:
time: 440 us; the launch traced here: 439 us
  waiting for transfers between devices  364 us (83%)
  blocking collectives  33.3 us (8%)
  matrix products  17.7 us (4%)
  between operations  13.8 us (3%)
  other arithmetic  10.8 us (2%)
    psum x1, waiting for transfers between devices, broadcast(): return lax.psum(block, axis)  182 us
    reduce_scatter x1, waiting for transfers between devices, per_device(): lax.psum_scatter(lax.dot_general(mirrored, inverse_tile, (((0,), (1,)), (...  102 us
    all_gather x1, waiting for transfers between devices, per_device(): wide_rows = lax.all_gather(lhat_flat, 'pcol', axis=1, tiled=True)  80.2 us
    psum x1, blocking collectives, per_device(): lax.psum(partial_diag.astype(jnp.bfloat16), 'prow').astype(jnp.float32)  33.3 us
    dot_general x1, matrix products, per_device(): lax.dot_general(mirrored, inverse_tile, (((0,), (1,)), ((), ())), preferr...  14 us
  transfers between devices with their start and end apart: 3, of which 3 were waited for; matrix products, arithmetic and copies ran while one was open for 0% of the time, Pallas kernels for 0%

commit v1 on v0

v1 whole, which is shorter than its diff:
```python
import jax
import jax.numpy as jnp
from jax import lax
from jax.experimental import pallas as pl
from jax.experimental.pallas import tpu as pltpu
from jax.sharding import PartitionSpec as P

MESH = pl.DeviceIdType.MESH
BLOCK = 128
ORDER = (2, 1, 3, 0)
F32 = jnp.float32
BF16 = jnp.bfloat16


def device(x, y, z, core):
    return ((y % 2) * 4 + x, (y // 2) * 8 + z * 2 + core)


def kernel(
    listed, panel_hbm, tile_hbm, unit, pivot, out, diag_out,
    panel, lhat, tile, mirrored, held, s2, r2, s1, r1, s3, r3, p1, p0, y_send, y_recv,
    kept, split, d_send, d_recv,
    local_sem, core_sem, t_send, t_recv, ye_send, ye_recv, x_send, x_recv, f_send, f_recv,
    z_send, z_recv, yr_send, yr_recv, dg_send, dg_recv,
):
    row, col = lax.axis_index("prow"), lax.axis_index("pcol")
    x, y_lo = row % 4, row // 4
    y_hi, z, core = col // 8, (col // 2) % 4, col % 2
    y = 2 * y_hi + y_lo
    y_swap = 2 * y_lo + y_hi
    rows = panel.shape[0]
    half, quarter, eighth = rows // 2, rows // 4, rows // 8
    blocks = rows // BLOCK

    load_panel = pltpu.make_async_copy(panel_hbm, panel, local_sem.at[0])
    load_panel.start()
    load_tile = pltpu.make_async_copy(tile_hbm, tile.at[core], local_sem.at[1])
    load_tile.start()

    def remote(src, dst, send, recv, to):
        return pltpu.make_async_remote_copy(
            src_ref=src, dst_ref=dst, send_sem=send, recv_sem=recv, device_id=to, device_id_type=MESH
        )

    barrier = pltpu.get_barrier_semaphore()

    def greet(to):
        pl.semaphore_signal(barrier, inc=1, device_id=to, device_id_type=MESH)

    x_next, x_prev = device((x + 1) % 4, y, z, core), device((x + 3) % 4, y, z, core)
    z_next, z_prev = device(x, y, (z + 1) % 4, core), device(x, y, (z + 3) % 4, core)
    y_pair = device(x, 2 * y_hi + 1 - y_lo, z, core)
    y_far = device(x, 2 * (1 - y_hi) + y_lo, z, core)
    other_core = device(x, y, z, 1 - core)
    for step in range(1, 8):
        greet(((row + step) % 8, col))
    for to in (z_next, z_prev, y_far, other_core):
        greet(to)
    for q in range(4):
        greet(device(q, y_swap, x, core))
        greet(device(z, y_swap, q, core))

    load_panel.wait()

    def lhat_block(b, carry):
        at = pl.ds(pl.multiple_of(b * BLOCK, BLOCK), BLOCK)
        mask = listed[col, row * blocks + b].astype(F32)
        masked = (panel[at, :].astype(F32) * mask).astype(BF16)
        lhat[at, :] = jnp.dot(masked, unit[0], preferred_element_type=F32).astype(BF16)
        return carry

    lax.fori_loop(0, blocks, lhat_block, 0)
    pl.semaphore_wait(barrier, 19)

    d_mine = (x + 4 - z) % 4

    def t_copy(q):
        at = pl.ds(q * quarter, quarter)
        return (
            remote(lhat.at[at], mirrored.at[d_mine, y_hi, at], t_send.at[q], t_recv.at[d_mine], device(q, y_swap, x, core)),
            jnp.logical_and(jnp.logical_and(q == x, y_swap == y), x == z),
            at,
        )

    for q in range(4):
        copy, same, at = t_copy(q)

        @pl.when(jnp.logical_not(same))
        def _():
            copy.start()

        @pl.when(same)
        def _():
            mine = pltpu.make_async_copy(lhat.at[at], mirrored.at[d_mine, y_hi, at], local_sem.at[2])
            mine.start()
            mine.wait()

    swap = remote(tile_hbm, tile.at[core], core_sem.at[0], core_sem.at[1], other_core)
    swap.start()

    def quarter_of(d, e, q, part=None):
        if part is None:
            at = pl.ds(pl.multiple_of(q * quarter, quarter), quarter)
        else:
            at = pl.ds(pl.multiple_of(q * quarter + part * eighth, eighth), eighth)
        return mirrored.at[d, e, at]

    lane = (y_lo, 1 - y_lo)
    x_left, x_right, x_far = (x + 3) % 4, (x + 1) % 4, (x + 2) % 4

    def y_copy(d):
        mine = quarter_of(d, lane[0], x)
        return remote(mine, mine, ye_send.at[d], ye_recv.at[d], y_pair)

    def x_copy(d, ab, side):
        mine = quarter_of(d, lane[ab], x)
        to = (x_next, x_prev)[side]
        return remote(mine, mine, x_send.at[d, ab, side], x_recv.at[d, ab, side], to)

    def f_copy(d, ab, side):
        relayed = quarter_of(d, lane[ab], (x_left, x_right)[side], side)
        to = (x_next, x_prev)[side]
        return remote(relayed, relayed, f_send.at[d, ab, side], f_recv.at[d, ab, side], to)

    def arrival(ref, sem):
        return remote(ref, ref, core_sem.at[0], sem, x_next)

    def send_first(d):
        first = quarter_of(d, lane[0], x)
        if d == 0:
            own = jnp.logical_and(y_swap == y, x == z)

            @pl.when(jnp.logical_not(own))
            def _():
                arrival(first, t_recv.at[d]).wait_recv()
        else:
            arrival(first, t_recv.at[d]).wait_recv()
        y_copy(d).start()
        x_copy(d, 0, 0).start()
        x_copy(d, 0, 1).start()

    def send_second(d):
        arrival(quarter_of(d, lane[1], x), ye_recv.at[d]).wait_recv()
        x_copy(d, 1, 0).start()
        x_copy(d, 1, 1).start()

    def relay(d):
        for ab in range(2):
            for side in range(2):
                arrival(quarter_of(d, lane[ab], (x_left, x_right)[side]), x_recv.at[d, ab, side]).wait_recv()
                f_copy(d, ab, side).start()

    def complete(d):
        for ab in range(2):
            for side in range(2):
                arrival(quarter_of(d, lane[ab], x_far, side), f_recv.at[d, ab, side]).wait_recv()

    step_n = 512

    def product(d, start, count, store):
        def body(i, carry):
            at = pl.ds(pl.multiple_of(start + i * step_n, step_n), step_n)
            acc = None
            for k in range(2):
                rhs = jnp.concatenate(
                    [mirrored[d, 0, k * half:(k + 1) * half, :], mirrored[d, 1, k * half:(k + 1) * half, :]], axis=1
                )
                term = jnp.dot(tile[k, at, :], rhs, preferred_element_type=F32)
                acc = term if acc is None else acc + term
            store(i, at, acc)
            return carry

        lax.fori_loop(0, count // step_n, body, 0)

    def z_copy(which, h):
        at = pl.ds(h * half, half)
        src, dst = ((s2, r2), (s1, r1), (s3, r3))[which]
        to = (z_prev, z_next)[h] if which == 0 else (None, z_prev, z_next)[which]
        return remote(src.at[:, at], dst.at[:, at], z_send.at[which, h], z_recv.at[which, h], to)

    def z_arrival(which, h):
        at = pl.ds(h * half, half)
        dst = (r2, r1, r3)[which]
        arrival(dst.at[:, at], z_recv.at[which, h]).wait_recv()

    def into(ref):
        def store(i, at, acc):
            ref[0, at, :] = acc[:, :BLOCK].astype(ref.dtype)
            ref[1, at, :] = acc[:, BLOCK:].astype(ref.dtype)

        return store

    def into_p1(i, at, acc):
        low = pl.ds(pl.multiple_of(i * step_n, step_n), step_n)
        p1[0, low, :] = acc[:, :BLOCK]
        p1[1, low, :] = acc[:, BLOCK:]

    def into_s3_added(i, at, acc):
        s3[0, at, :] = (acc[:, :BLOCK] + r2[0, at, :].astype(F32)).astype(BF16)
        s3[1, at, :] = (acc[:, BLOCK:] + r2[1, at, :].astype(F32)).astype(BF16)

    d0, d1, d2, d3 = ORDER
    send_first(d0)
    send_first(d1)
    send_second(d0)
    relay(d0)
    send_second(d1)
    send_first(d2)
    load_tile.wait()
    swap.wait_recv()
    complete(d0)
    product(d0, 0, half, into(s2))
    z_copy(0, 0).start()
    product(d0, half, half, into(s2))
    z_copy(0, 1).start()

    relay(d1)
    send_second(d2)
    send_first(d3)
    complete(d1)
    product(d1, half, half, into(s1))
    z_copy(1, 1).start()
    product(d1, 0, half, into_p1)

    relay(d2)
    send_second(d3)
    z_arrival(0, 0)
    for e in range(2):
        s1[e, 0:half, :] = (p1[e] + r2[e, 0:half, :].astype(F32)).astype(BF16)
    z_copy(1, 0).start()
    complete(d2)
    z_arrival(0, 1)
    product(d2, half, half, into_s3_added)
    z_copy(2, 1).start()
    product(d2, 0, half, into(s3))
    z_copy(2, 0).start()

    relay(d3)
    complete(d3)
    product(d3, 0, rows, into(p0))

    def y_reduce(h):
        at = pl.ds(h * half, half)
        return remote(y_send.at[at], y_recv.at[at], yr_send.at[h], yr_recv.at[h], y_far)

    for h in (1, 0):
        at = pl.ds(h * half, half)
        z_arrival(1, h)
        z_arrival(2, h)
        e = 1 - y_hi
        y_send[at, :] = (p0[e, at, :] + (r1[e, at, :].astype(F32) + r3[e, at, :].astype(F32))).astype(BF16)
        y_reduce(h).start()
        e = y_hi
        kept[at, :] = p0[e, at, :] + (r1[e, at, :].astype(F32) + r3[e, at, :].astype(F32))

    total = None
    for h in (1, 0):
        arrival(y_recv.at[pl.ds(h * half, half)], yr_recv.at[h]).wait_recv()

        def finish(b, carry):
            at = pl.ds(pl.multiple_of(b * BLOCK, BLOCK), BLOCK)
            value = (kept[at, :] + y_recv[at, :].astype(F32)).T
            mask = listed[col, row * blocks + b].astype(F32)
            out[:, at] = -(value * mask)
            high = value.astype(BF16)
            split[0:BLOCK, at] = high
            split[BLOCK:, at] = (value - high.astype(F32)).astype(BF16)
            return carry

        lax.fori_loop(h * (blocks // 2), (h + 1) * (blocks // 2), finish, 0)
        at = pl.ds(h * half, half)
        both = jnp.dot(split[:, h * half:(h + 1) * half], lhat[at, :], preferred_element_type=F32)
        part = both[0:BLOCK] + both[BLOCK:]
        total = part if total is None else total + part

    d_send[...] = total.astype(BF16)

    def d_copy(step):
        to = (row + step) % 8
        return remote(d_send, d_recv.at[row], dg_send.at[step - 1], dg_recv.at[step - 1], (to, col))

    for step in range(1, 8):
        d_copy(step).start()
    d_recv[row] = d_send[...]
    for step in range(1, 8):
        arrival(d_recv.at[(row + 8 - step) % 8], dg_recv.at[step - 1]).wait_recv()
    total = d_recv[0].astype(F32)
    for other in range(1, 8):
        total = total + d_recv[other].astype(F32)
    diag_out[0] = pivot[0] + total

    swap.wait_send()
    for q in range(4):
        copy, same, at = t_copy(q)

        @pl.when(jnp.logical_not(same))
        def _():
            copy.wait_send()

    for d in range(4):
        y_copy(d).wait_send()
        for ab in range(2):
            for side in range(2):
                x_copy(d, ab, side).wait_send()
                f_copy(d, ab, side).wait_send()
    for which in range(3):
        for h in range(2):
            z_copy(which, h).wait_send()
    for h in range(2):
        y_reduce(h).wait_send()
    for step in range(1, 8):
        d_copy(step).wait_send()


def per_device(l_panel, inverse_tile, unit_inverse, pivot_inverse, listed):
    rows, width = l_panel.shape
    columns = inverse_tile.shape[1]
    dma = pltpu.SemaphoreType.DMA
    vmem = pl.BlockSpec(memory_space=pltpu.VMEM)
    hbm = pl.BlockSpec(memory_space=pltpu.HBM)
    pair = (2, rows, width)
    return pl.pallas_call(
        kernel,
        out_shape=(
            jax.ShapeDtypeStruct((width, rows), F32),
            jax.ShapeDtypeStruct((1, width, width), F32),
        ),
        in_specs=[pl.BlockSpec(memory_space=pltpu.SMEM), hbm, hbm, vmem, vmem],
        out_specs=(vmem, vmem),
        scratch_shapes=[
            pltpu.VMEM((rows, width), BF16),
            pltpu.VMEM((rows, width), BF16),
            pltpu.VMEM((2, rows, columns), BF16),
            pltpu.VMEM((4, 2, rows, width), BF16),
            pltpu.VMEM((8, width), BF16),
            pltpu.VMEM(pair, BF16),
            pltpu.VMEM(pair, BF16),
            pltpu.VMEM(pair, BF16),
            pltpu.VMEM(pair, BF16),
            pltpu.VMEM(pair, BF16),
            pltpu.VMEM(pair, BF16),
            pltpu.VMEM((2, rows // 2, width), F32),
            pltpu.VMEM(pair, F32),
            pltpu.VMEM((rows, width), BF16),
            pltpu.VMEM((rows, width), BF16),
            pltpu.VMEM((rows, width), F32),
            pltpu.VMEM((2 * width, rows), BF16),
            pltpu.VMEM((width, width), BF16),
            pltpu.VMEM((8, width, width), BF16),
            dma((3,)),
            dma((2,)),
            dma((4,)),
            dma((4,)),
            dma((4,)),
            dma((4,)),
            dma((4, 2, 2)),
            dma((4, 2, 2)),
            dma((4, 2, 2)),
            dma((4, 2, 2)),
            dma((3, 2)),
            dma((3, 2)),
            dma((2,)),
            dma((2,)),
            dma((7,)),
            dma((7,)),
        ],
        compiler_params=pltpu.CompilerParams(
            collective_id=0, has_side_effects=True, vmem_limit_bytes=48 << 20
        ),
    )(listed, l_panel, inverse_tile, unit_inverse, pivot_inverse)


def solution(mesh):
    return jax.shard_map(
        per_device,
        mesh=mesh,
        in_specs=(
            P("prow", "pcol"),
            P("prow", "pcol"),
            P("pcol", None, None),
            P("pcol", None, None),
            P(),
        ),
        out_specs=(P("pcol", "prow"), P("pcol", None, None)),
        check_vma=False,
    )
```

time: 440 us -> 102 us (0.23)
  waiting for transfers between devices: 364 us -> 0 us
  Pallas kernels: 0 us -> 93.9 us
  blocking collectives: 33.3 us -> 0 us
  matrix products: 17.7 us -> 0 us
  between operations: 13.8 us -> 0.65 us
  other arithmetic: 10.8 us -> 0 us
  local copies, waits for them, and re-layouts: 0.02 us -> 7.12 us
    psum x1 -> x0, waiting for transfers between devices: 182 us -> none  [broadcast(): return lax.psum(block, axis)]
    reduce_scatter x1 -> x0, waiting for transfers between devices: 102 us -> none  [per_device(): lax.psum_scatter(lax.dot_general(mirrored, inverse_tile, (((0,), (1,)), (...]
    pallas_call x0 -> x1, Pallas kernels: none -> 93.9 us  [per_device(): pl.pallas_call(kernel, out_shape=(jax.ShapeDtypeStruct((width, rows), F32...]
    all_gather x1 -> x0, waiting for transfers between devices: 80.2 us -> none  [per_device(): wide_rows = lax.all_gather(lhat_flat, 'pcol', axis=1, tiled=True)]
    psum x1 -> x0, blocking collectives: 33.3 us -> none  [per_device(): lax.psum(partial_diag.astype(jnp.bfloat16), 'prow').astype(jnp.float32)]
    dot_general x3 -> x0, matrix products: 17.7 us -> none  [the longest x1 14 us: per_device(): lax.dot_general(mirrored, inverse_tile, (((0,), (1,)), ((), ())), preferr...]
    select_n x1 -> x0, other arithmetic: 7.14 us -> none  [broadcast(): jnp.where(lax.axis_index(axis) == source, block, jnp.zeros_like(block))]
    unnamed x6 -> x12, local copies, waits for them, and re-layouts: 0.02 us -> 7.12 us
  transfers between devices with their start and end apart: 3 -> 0, of which waited for: 3 -> 0; matrix products, arithmetic and copies ran while one was open for 0% -> 0% of each run, Pallas kernels for 0% -> 0%
where the time goes in v1:
time: 102 us
  Pallas kernels  93.9 us (92%)
  local copies, waits for them, and re-layouts  7.12 us (7%)
    pallas_call x1, Pallas kernels, per_device(): pl.pallas_call(kernel, out_shape=(jax.ShapeDtypeStruct((width, rows), F32...  93.9 us
    unnamed x12, local copies, waits for them, and re-layouts  7.12 us

profile of v1, /device:TPU:0, one launch (start us, length us, event | category | flops | bytes accessed | tf_op | source)
XLA Modules:
  0.0 101.7 jit_solution(1552401761139837425)
XLA Ops:
  0.6 0.0 copy-start
  0.6 2.2 %copy-done = bf16[2048,1024]{1,0:T(8,128)(2,1)S(1)} copy-done((bf16[2048,1024]{1,0:T(8,128)(2,1)S(1)}, bf16[2048,1024]{1,0:T(8,128)(2,1)}, u32[]{:S(2)}) %copy-start) | copy-done | bytes 4194328
  2.8 0.0 copy-start.1
  2.8 1.0 %copy-done.1 = bf16[2048,128]{1,0:T(8,128)(2,1)S(1)} copy-done((bf16[2048,128]{1,0:T(8,128)(2,1)S(1)}, bf16[2048,128]{1,0:T(8,128)(2,1)}, u32[]{:S(2)}) %copy-start.1) | copy-done | bytes 524312
  3.9 0.0 copy-start.2
  3.9 0.8 copy-done.2
  4.7 0.0 copy-start.3
  4.7 0.8 copy-done.3
  5.5 0.0 copy-start.4
  5.5 0.7 copy-done.4
  6.2 93.9 %shard_map.68 = (f32[128,2048]{1,0:T(8,128)S(1)}, f32[1,128,128]{2,1,0:T(8,128)S(1)}) custom-call(s32[16,128]{1,0:T(8,128)S(1)} %copy-done.4, bf16[2048,128]{1,0:T(8,128)(2,1)S(1)} %copy-done.1, bf16[2048,1024]{1,0:T(8,128)(2,1)S(1)} %copy-done, bf16[1,128,128]{2,1,0:T(8,128)(2,1)S(1)} %copy-done.3, f32[1,128,128]{2,1,0:T(8,128)S(1)} %copy-done.2), custom_call_target="tpu_custom_call" | custom-call | tf_op jit(solution)/shard_map/pallas_call | solution.py:322
  100.1 1.0 copy.9
  101.1 0.6 copy.10
Async XLA Ops:
  0.6 2.2 %copy-start = (bf16[2048,1024]{1,0:T(8,128)(2,1)S(1)}, bf16[2048,1024]{1,0:T(8,128)(2,1)}, u32[]{:S(2)}) copy-start(bf16[2048,1024]{1,0:T(8,128)(2,1)} %tile_hbm.1) | copy-start | bytes 12582916
  2.8 1.0 %copy-start.1 = (bf16[2048,128]{1,0:T(8,128)(2,1)S(1)}, bf16[2048,128]{1,0:T(8,128)(2,1)}, u32[]{:S(2)}) copy-start(bf16[2048,128]{1,0:T(8,128)(2,1)} %panel_hbm.1) | copy-start | bytes 1572868
  3.9 0.8 copy-start.2
  4.7 0.8 copy-start.3
  5.5 0.7 copy-start.4

commit v2 on v1

v2 whole, which is shorter than its diff:
```python
import jax
import jax.numpy as jnp
from jax import lax
from jax.experimental import pallas as pl
from jax.experimental.pallas import tpu as pltpu
from jax.sharding import PartitionSpec as P

MESH = pl.DeviceIdType.MESH
BLOCK = 128
CHUNKS = ((2, 0), (2, 1), (1, 1), (3, 1), (1, 0), (3, 0), (0, 1), (0, 0))
F32 = jnp.float32
BF16 = jnp.bfloat16


def device(x, y, z, core):
    return ((y % 2) * 4 + x, (y // 2) * 8 + z * 2 + core)


def kernel(
    listed_hbm, panel_hbm, tile_hbm, unit_hbm, pivot_hbm, out, diag_out,
    listed, unit, pivot, panel, lhat, tile, mirrored, s2, r2, s1, r1, s3, r3, p1, p3, p0, y_send, y_recv,
    split, d_send, d_recv,
    local_sem, core_sem, t_send, in_recv, ye_send, x_send, x_recv, f_send, f_recv,
    z_send, z_recv, yr_send, yr_recv, dg_send, dg_recv,
):
    row, col = lax.axis_index("prow"), lax.axis_index("pcol")
    x, y_lo = row % 4, row // 4
    y_hi, z, core = col // 8, (col // 2) % 4, col % 2
    y = 2 * y_hi + y_lo
    y_swap = 2 * y_lo + y_hi
    rows = panel.shape[0]
    half, quarter, eighth = rows // 2, rows // 4, rows // 8
    blocks = rows // BLOCK

    loads = [
        pltpu.make_async_copy(src, dst, local_sem.at[i])
        for i, (src, dst) in enumerate(
            (
                (panel_hbm, panel),
                (listed_hbm, listed),
                (unit_hbm, unit),
                (tile_hbm, tile.at[core]),
                (pivot_hbm, pivot),
            )
        )
    ]
    for load in loads:
        load.start()

    def remote(src, dst, send, recv, to):
        return pltpu.make_async_remote_copy(
            src_ref=src, dst_ref=dst, send_sem=send, recv_sem=recv, device_id=to, device_id_type=MESH
        )

    barrier = pltpu.get_barrier_semaphore()

    def greet(to):
        pl.semaphore_signal(barrier, inc=1, device_id=to, device_id_type=MESH)

    x_next, x_prev = device((x + 1) % 4, y, z, core), device((x + 3) % 4, y, z, core)
    z_next, z_prev = device(x, y, (z + 1) % 4, core), device(x, y, (z + 3) % 4, core)
    y_pair = device(x, 2 * y_hi + 1 - y_lo, z, core)
    y_far = device(x, 2 * (1 - y_hi) + y_lo, z, core)
    other_core = device(x, y, z, 1 - core)
    for step in range(1, 8):
        greet(((row + step) % 8, col))
    for to in (z_next, z_prev, y_far, other_core):
        greet(to)
    for q in range(4):
        greet(device(q, y_swap, x, core))
        greet(device(z, y_swap, q, core))

    for load in loads[:3]:
        load.wait()

    def lhat_block(b, carry):
        at = pl.ds(pl.multiple_of(b * BLOCK, BLOCK), BLOCK)
        mask = listed[col, row * blocks + b].astype(F32)
        masked = (panel[at, :].astype(F32) * mask).astype(BF16)
        lhat[at, :] = jnp.dot(masked, unit[0], preferred_element_type=F32).astype(BF16)
        return carry

    lax.fori_loop(0, blocks, lhat_block, 0)
    pl.semaphore_wait(barrier, 19)

    d_mine = (x + 4 - z) % 4

    def t_copy(q):
        at = pl.ds(q * quarter, quarter)
        same = jnp.logical_and(jnp.logical_and(q == x, y_swap == y), x == z)
        src, dst, sem = lhat.at[at], mirrored.at[d_mine, y_hi, at], in_recv.at[d_mine, y_hi]
        return remote(src, dst, t_send.at[q], sem, device(q, y_swap, x, core)), same, (src, dst, sem)

    for q in range(4):
        copy, same, (src, dst, sem) = t_copy(q)

        @pl.when(jnp.logical_not(same))
        def _():
            copy.start()

        @pl.when(same)
        def _():
            pltpu.make_async_copy(src, dst, sem).start()

    swap = remote(tile_hbm, tile.at[core], core_sem.at[0], core_sem.at[1], other_core)
    swap.start()

    def quarter_of(d, e, q, part=None):
        if part is None:
            at = pl.ds(pl.multiple_of(q * quarter, quarter), quarter)
        else:
            at = pl.ds(pl.multiple_of(q * quarter + part * eighth, eighth), eighth)
        return mirrored.at[d, e, at]

    lane = (y_hi, 1 - y_hi)
    x_left, x_right, x_far = (x + 3) % 4, (x + 1) % 4, (x + 2) % 4

    def y_copy(d, nf):
        mine = quarter_of(d, lane[nf], x)
        return remote(mine, mine, ye_send.at[d], in_recv.at[d, lane[nf]], y_pair)

    def x_copy(d, nf, side):
        mine = quarter_of(d, lane[nf], x)
        to = (x_next, x_prev)[side]
        return remote(mine, mine, x_send.at[d, nf, side], x_recv.at[d, nf, side], to)

    def f_copy(d, nf, side):
        relayed = quarter_of(d, lane[nf], (x_left, x_right)[side], side)
        to = (x_next, x_prev)[side]
        return remote(relayed, relayed, f_send.at[d, nf, side], f_recv.at[d, nf, side], to)

    def arrival(ref, sem):
        return remote(ref, ref, core_sem.at[0], sem, x_next)

    def enter(d, nf):
        arrival(quarter_of(d, lane[nf], x), in_recv.at[d, lane[nf]]).wait_recv()

        @pl.when(y_lo == lane[nf])
        def _():
            y_copy(d, nf).start()

        x_copy(d, nf, 0).start()
        x_copy(d, nf, 1).start()

    def relay(d, nf):
        for side in range(2):
            arrival(quarter_of(d, lane[nf], (x_left, x_right)[side]), x_recv.at[d, nf, side]).wait_recv()
            f_copy(d, nf, side).start()

    def complete(d, nf):
        for side in range(2):
            arrival(quarter_of(d, lane[nf], x_far, side), f_recv.at[d, nf, side]).wait_recv()

    step_n = 512

    def product(d, nf, start, count, store):
        def body(i, carry):
            at = pl.ds(pl.multiple_of(start + i * step_n, step_n), step_n)
            acc = None
            for k in range(2):
                rhs = mirrored[d, lane[nf], k * half:(k + 1) * half, :]
                term = jnp.dot(tile[k, at, :], rhs, preferred_element_type=F32)
                acc = term if acc is None else acc + term
            store(i, at, acc)
            return carry

        lax.fori_loop(0, count // step_n, body, 0)

    sides = {2: (s2, r2), 1: (s1, r1), 3: (s3, r3)}

    def z_copy(d, nf, h):
        at = pl.ds(h * half, half)
        src, dst = sides[d]
        to = (z_prev, z_next)[h] if d == 2 else (z_prev if d == 1 else z_next)
        return remote(src.at[nf, at], dst.at[nf, at], z_send.at[d - 1, nf, h], z_recv.at[d - 1, nf, h], to)

    def z_arrival(d, nf, h):
        arrival(sides[d][1].at[nf, pl.ds(h * half, half)], z_recv.at[d - 1, nf, h]).wait_recv()

    def into(ref, nf):
        def store(i, at, acc):
            ref[nf, at, :] = acc.astype(ref.dtype)

        return store

    def into_half(ref, nf):
        def store(i, at, acc):
            ref[nf, pl.ds(pl.multiple_of(i * step_n, step_n), step_n), :] = acc

        return store

    def compute(d, nf):
        if d == 2:
            for h in range(2):
                product(d, nf, h * half, half, into(s2, nf))
                z_copy(d, nf, h).start()
        elif d == 1:
            product(d, nf, half, half, into(s1, nf))
            z_copy(d, nf, 1).start()
            product(d, nf, 0, half, into_half(p1, nf))
        elif d == 3:
            product(d, nf, 0, half, into(s3, nf))
            z_copy(d, nf, 0).start()
            product(d, nf, half, half, into_half(p3, nf))
        else:
            product(d, nf, 0, rows, into(p0, nf))

    def add_far(d, nf):
        h = 0 if d == 1 else 1
        at = pl.ds(h * half, half)
        z_arrival(2, nf, h)
        held = p1 if d == 1 else p3
        sides[d][0][nf, at, :] = (held[nf] + r2[nf, at, :].astype(F32)).astype(BF16)
        z_copy(d, nf, h).start()

    enter(*CHUNKS[0])
    enter(*CHUNKS[1])
    for i, (d, nf) in enumerate(CHUNKS):
        relay(d, nf)
        if i + 2 < len(CHUNKS):
            enter(*CHUNKS[i + 2])
        if i == 0:
            loads[3].wait()
            swap.wait_recv()
        if i == 4:
            add_far(1, 1)
            add_far(3, 1)
        if i == 7:
            for h in range(2):
                z_arrival(1, 1, h)
                z_arrival(3, 1, h)
            y_send[...] = (p0[1] + (r1[1].astype(F32) + r3[1].astype(F32))).astype(BF16)
            y_reduce = remote(y_send, y_recv, yr_send.at[0], yr_recv.at[0], y_far)
            y_reduce.start()
        complete(d, nf)
        compute(d, nf)
        if (d, nf) in ((1, 0), (3, 0)):
            add_far(d, nf)

    for h in (1, 0):
        z_arrival(1, 0, h)
        z_arrival(3, 0, h)
    arrival(y_recv, yr_recv.at[0]).wait_recv()

    def finish(b, carry):
        at = pl.ds(pl.multiple_of(b * BLOCK, BLOCK), BLOCK)
        value = (p0[0, at, :] + y_recv[at, :].astype(F32)) + (r1[0, at, :].astype(F32) + r3[0, at, :].astype(F32))
        value = value.T
        mask = listed[col, row * blocks + b].astype(F32)
        out[:, at] = -(value * mask)
        high = value.astype(BF16)
        split[0:BLOCK, at] = high
        split[BLOCK:, at] = (value - high.astype(F32)).astype(BF16)
        return carry

    lax.fori_loop(0, blocks, finish, 0)
    both = jnp.dot(split[...], lhat[...], preferred_element_type=F32)
    total = both[0:BLOCK] + both[BLOCK:]
    d_send[...] = total.astype(BF16)

    def d_copy(step):
        to = (row + step) % 8
        return remote(d_send, d_recv.at[row], dg_send.at[step - 1], dg_recv.at[step - 1], (to, col))

    for step in range(1, 8):
        d_copy(step).start()
    d_recv[row] = d_send[...]
    for step in range(1, 8):
        arrival(d_recv.at[(row + 8 - step) % 8], dg_recv.at[step - 1]).wait_recv()
    total = d_recv[0].astype(F32)
    for other in range(1, 8):
        total = total + d_recv[other].astype(F32)
    loads[4].wait()
    diag_out[0] = pivot[0] + total

    swap.wait_send()
    for q in range(4):
        copy, same, _ = t_copy(q)

        @pl.when(jnp.logical_not(same))
        def _():
            copy.wait_send()

    for d, nf in CHUNKS:

        @pl.when(y_lo == lane[nf])
        def _():
            y_copy(d, nf).wait_send()

        for side in range(2):
            x_copy(d, nf, side).wait_send()
            f_copy(d, nf, side).wait_send()
            if d:
                z_copy(d, nf, side).wait_send()
    y_reduce.wait_send()
    for step in range(1, 8):
        d_copy(step).wait_send()


def per_device(l_panel, inverse_tile, unit_inverse, pivot_inverse, listed):
    rows, width = l_panel.shape
    columns = inverse_tile.shape[1]
    dma = pltpu.SemaphoreType.DMA
    vmem = pl.BlockSpec(memory_space=pltpu.VMEM)
    hbm = pl.BlockSpec(memory_space=pltpu.HBM)
    pair = (2, rows, width)
    operands = (listed, l_panel, inverse_tile, unit_inverse, pivot_inverse)
    return pl.pallas_call(
        kernel,
        out_shape=(
            jax.ShapeDtypeStruct((width, rows), F32),
            jax.ShapeDtypeStruct((1, width, width), F32),
        ),
        in_specs=[hbm] * 5,
        out_specs=(vmem, vmem),
        scratch_shapes=[
            pltpu.SMEM(listed.shape, jnp.int32),
            pltpu.VMEM((1, width, width), BF16),
            pltpu.VMEM((1, width, width), F32),
            pltpu.VMEM((rows, width), BF16),
            pltpu.VMEM((rows, width), BF16),
            pltpu.VMEM((2, rows, columns), BF16),
            pltpu.VMEM((4, 2, rows, width), BF16),
            pltpu.VMEM(pair, BF16),
            pltpu.VMEM(pair, BF16),
            pltpu.VMEM(pair, BF16),
            pltpu.VMEM(pair, BF16),
            pltpu.VMEM(pair, BF16),
            pltpu.VMEM(pair, BF16),
            pltpu.VMEM((2, rows // 2, width), F32),
            pltpu.VMEM((2, rows // 2, width), F32),
            pltpu.VMEM(pair, F32),
            pltpu.VMEM((rows, width), BF16),
            pltpu.VMEM((rows, width), BF16),
            pltpu.VMEM((2 * width, rows), BF16),
            pltpu.VMEM((width, width), BF16),
            pltpu.VMEM((8, width, width), BF16),
            dma((5,)),
            dma((2,)),
            dma((4,)),
            dma((4, 2)),
            dma((4,)),
            dma((4, 2, 2)),
            dma((4, 2, 2)),
            dma((4, 2, 2)),
            dma((4, 2, 2)),
            dma((3, 2, 2)),
            dma((3, 2, 2)),
            dma((1,)),
            dma((1,)),
            dma((7,)),
            dma((7,)),
        ],
        compiler_params=pltpu.CompilerParams(
            collective_id=0, has_side_effects=True, vmem_limit_bytes=60 << 20
        ),
    )(*(pltpu.with_memory_space_constraint(a, pltpu.HBM) for a in operands))


def solution(mesh):
    return jax.shard_map(
        per_device,
        mesh=mesh,
        in_specs=(
            P("prow", "pcol"),
            P("prow", "pcol"),
            P("pcol", None, None),
            P("pcol", None, None),
            P(),
        ),
        out_specs=(P("pcol", "prow"), P("pcol", None, None)),
        check_vma=False,
    )
```

time: 102 us -> 105 us (1.029)
  Pallas kernels: 93.9 us -> 101 us
  local copies, waits for them, and re-layouts: 7.12 us -> 3.77 us
    pallas_call x1, Pallas kernels: 93.9 us -> 101 us  [per_device(): pl.pallas_call(kernel, out_shape=(jax.ShapeDtypeStruct((width, rows), F32...]
    unnamed x12 -> x2, local copies, waits for them, and re-layouts: 7.12 us -> 3.77 us
where the time goes in v2:
time: 105 us
  Pallas kernels  101 us (96%)
  local copies, waits for them, and re-layouts  3.77 us (4%)
    pallas_call x1, Pallas kernels, per_device(): pl.pallas_call(kernel, out_shape=(jax.ShapeDtypeStruct((width, rows), F32...  101 us
    unnamed x2, local copies, waits for them, and re-layouts  3.77 us

profile of v2, /device:TPU:0, one launch (start us, length us, event | category | flops | bytes accessed | tf_op | source)
XLA Modules:
  0.0 105.1 jit_solution(13242050106981170882)
XLA Ops:
  0.6 100.7 %shard_map.68 = (f32[128,2048]{1,0:T(8,128)}, f32[1,128,128]{2,1,0:T(8,128)}) custom-call(s32[16,128]{1,0:T(8,128)} %listed_hbm.1, bf16[2048,128]{1,0:T(8,128)(2,1)} %panel_hbm.1, bf16[2048,1024]{1,0:T(8,128)(2,1)} %tile_hbm.1, bf16[1,128,128]{2,1,0:T(8,128)(2,1)} %unit_hbm.1, f32[1,128,128]{2,1,0:T(8,128)} %pivot_hbm.1), custom_call_target="tpu_custom_call" | custom-call | tf_op jit(solution)/shard_map/pallas_call | solution.py:308
  101.3 2.3 %copy.9 = f32[128,2048]{1,0:T(8,128)} copy(f32[128,2048]{1,0:T(8,128)} %get-tuple-element.4) | data formatting | bytes 2097152
  103.6 1.5 %copy.10 = f32[1,128,128]{2,1,0:T(8,128)} copy(f32[1,128,128]{2,1,0:T(8,128)} %get-tuple-element.5) | data formatting | bytes 131072

commit v3 on v0

v3 whole, which is shorter than its diff:
```python
import jax
import jax.numpy as jnp
from jax import lax
from jax.experimental import pallas as pl
from jax.experimental.pallas import tpu as pltpu
from jax.sharding import PartitionSpec as P

MESH = pl.DeviceIdType.MESH
BLOCK = 128
STEP = 512
ORDER = ((2, 0), (2, 1), (1, 1), (3, 1), (0, 1), (1, 0), (3, 0), (0, 0))
ADDED = {3: 2, 4: 3, 5: 5, 6: 6}
Y_AT = 7
F32 = jnp.float32
BF16 = jnp.bfloat16


def device(x, y, z, core):
    return ((y % 2) * 4 + x, (y // 2) * 8 + z * 2 + core)


def pick(index, table):
    value = table[-1]
    for at in range(len(table) - 2, -1, -1):
        value = jnp.where(index == at, table[at], value)
    return value


def chunk(index):
    return pick(index, [d for d, _ in ORDER]), pick(index, [nf for _, nf in ORDER])


def kernel(
    listed_hbm, panel_hbm, tile_hbm, unit_hbm, pivot_hbm, out, diag_out,
    listed, unit, pivot, panel, lhat, tile, mirrored, part, heard, y_send, y_recv,
    stage, split, d_send, d_recv,
    local_sem, core_sem, t_send, td_send, t_recv, in_recv, sw_send, ye_send,
    x_send, x_recv, f_send, f_recv, z_send, z_recv, yr_send, yr_recv, dg_send, dg_recv,
):
    row, col = lax.axis_index("prow"), lax.axis_index("pcol")
    x, y_lo = row % 4, row // 4
    y_hi, z, core = col // 8, (col // 2) % 4, col % 2
    y = 2 * y_hi + y_lo
    y_swap = 2 * y_lo + y_hi
    y_other = 2 * y_hi + 1 - y_lo
    stays = y_lo == y_hi
    moves = y_lo != y_hi
    rows = panel.shape[0]
    half, quarter, eighth = rows // 2, rows // 4, rows // 8
    blocks = rows // BLOCK

    loads = [
        pltpu.make_async_copy(src, dst, local_sem.at[i])
        for i, (src, dst) in enumerate(
            (
                (panel_hbm, panel),
                (listed_hbm, listed),
                (unit_hbm, unit),
                (tile_hbm, tile.at[core]),
                (pivot_hbm, pivot),
            )
        )
    ]
    for load in loads:
        load.start()

    def remote(src, dst, send, recv, to):
        return pltpu.make_async_remote_copy(
            src_ref=src, dst_ref=dst, send_sem=send, recv_sem=recv, device_id=to, device_id_type=MESH
        )

    def each(count, body):
        def step(i, carry):
            body(i)
            return carry

        lax.fori_loop(0, count, step, 0)

    def span(start, size):
        return pl.ds(pl.multiple_of(start, size), size)

    barrier = pltpu.get_barrier_semaphore()

    def greet(to):
        pl.semaphore_signal(barrier, inc=1, device_id=to, device_id_type=MESH)

    y_pair = device(x, y_other, z, core)
    y_far = device(x, 2 * (1 - y_hi) + y_lo, z, core)
    other_core = device(x, y, z, 1 - core)
    swapped = device(x, y_swap, z, core)
    for step in range(1, 8):
        greet(((row + step) % 8, col))
    for to in (device(x, y, (z + 1) % 4, core), device(x, y, (z + 3) % 4, core), y_far, other_core, swapped):
        greet(to)

    def greet_group(q):
        greet(device(q, y, x, core))
        greet(device(z, y, q, core))
        greet(device(q, y_other, x, core))
        greet(device(z, y_other, q, core))

    each(4, greet_group)

    for load in loads[:3]:
        load.wait()

    def lhat_block(b):
        at = span(b * BLOCK, BLOCK)
        mask = listed[col, row * blocks + b].astype(F32)
        masked = (panel[at, :].astype(F32) * mask).astype(BF16)
        lhat[at, :] = jnp.dot(masked, unit[0], preferred_element_type=F32).astype(BF16)

    each(blocks, lhat_block)
    pl.semaphore_wait(barrier, 28)

    d_mine = (x + 4 - z) % 4
    twice = jnp.logical_and(stays, d_mine == 2)

    def t_copy(q, straight):
        at = span(q * quarter, quarter)
        if straight:
            dst, sem = mirrored.at[d_mine, y_hi, at], in_recv.at[d_mine, y_hi]
        else:
            dst, sem = stage.at[d_mine], t_recv.at[d_mine]
        return remote(lhat.at[at], dst, t_send.at[q], sem, device(q, y, x, core)), (lhat.at[at], dst, sem)

    def t_twice(q):
        at = span(q * quarter, quarter)
        to = device(q, y_other, x, core)
        return remote(lhat.at[at], mirrored.at[2, y_hi, at], td_send.at[q], in_recv.at[2, y_hi], to)

    for straight, when in ((True, stays), (False, moves)):

        @pl.when(when)
        def _():
            @pl.when(x == z)
            def _():
                _, (src, dst, sem) = t_copy(x, straight)
                pltpu.make_async_copy(src, dst, sem).start()

            def send(q):
                @pl.when(jnp.logical_or(q != x, x != z))
                def _():
                    t_copy(q, straight)[0].start()

            each(4, send)

    @pl.when(twice)
    def _():
        each(4, lambda q: t_twice(q).start())

    swap = remote(tile_hbm, tile.at[core], core_sem.at[0], core_sem.at[1], other_core)
    swap.start()

    def quarter_of(d, e, q):
        return mirrored.at[d, e, span(q * quarter, quarter)]

    def eighth_of(d, e, q, side):
        return mirrored.at[d, e, span(q * quarter + side * eighth, eighth)]

    def lane(nf):
        return jnp.where(nf == 0, y_hi, 1 - y_hi)

    def side_x(side):
        return (x + 1 + 2 * side) % 4

    def from_x(side):
        return (x + 3 + 2 * side) % 4

    def swap_copy(d):
        return remote(stage.at[d], quarter_of(d, y_hi, x), sw_send.at[d], in_recv.at[d, y_hi], swapped)

    def y_copy(d):
        mine = quarter_of(d, y_lo, x)
        return remote(mine, mine, ye_send.at[d], in_recv.at[d, y_lo], y_pair)

    def x_copy(d, nf, side):
        mine = quarter_of(d, lane(nf), x)
        to = device(side_x(side), y, z, core)
        return remote(mine, mine, x_send.at[d, nf, side], x_recv.at[d, nf, side], to)

    def f_copy(d, nf, side):
        relayed = eighth_of(d, lane(nf), from_x(side), side)
        to = device(side_x(side), y, z, core)
        return remote(relayed, relayed, f_send.at[d, nf, side], f_recv.at[d, nf, side], to)

    def arrival(ref, sem):
        return remote(ref, ref, core_sem.at[0], sem, y_far)

    def y_sends(d):
        return jnp.logical_not(jnp.logical_and(stays, d == 2))

    def enter(index):
        d, nf = chunk(index)
        e = lane(nf)
        arrival(quarter_of(d, e, x), in_recv.at[d, e]).wait_recv()

        @pl.when(jnp.logical_and(y_lo == e, y_sends(d)))
        def _():
            y_copy(d).start()

        for side in range(2):
            x_copy(d, nf, side).start()

    def relay(index):
        d, nf = chunk(index)
        for side in range(2):
            arrival(quarter_of(d, lane(nf), from_x(side)), x_recv.at[d, nf, side]).wait_recv()
            f_copy(d, nf, side).start()

    def complete(d, nf):
        for side in range(2):
            arrival(eighth_of(d, lane(nf), (x + 2) % 4, side), f_recv.at[d, nf, side]).wait_recv()

    def z_copy(d, nf, h):
        at = span(h * half, half)
        down = jnp.logical_or(d == 1, jnp.logical_and(d == 2, h == 0))
        to = device(x, y, (z + jnp.where(down, 3, 1)) % 4, core)
        return remote(part.at[d, nf, at], heard.at[d - 1, nf, at], z_send.at[d, nf, h], z_recv.at[d - 1, nf, h], to)

    def z_arrival(d, nf, h):
        arrival(heard.at[d - 1, nf, span(h * half, half)], z_recv.at[d - 1, nf, h]).wait_recv()

    def y_reduce(h):
        at = span(h * half, half)
        return remote(y_send.at[at], y_recv.at[at], yr_send.at[h], yr_recv.at[h], y_far)

    def send_far(j):
        h = 1 - j
        z_arrival(1, 1, h)
        z_arrival(3, 1, h)

        def add(i):
            at = span(h * half + i * BLOCK, BLOCK)
            far = part[0, 1, at, :].astype(F32) + (heard[0, 1, at, :].astype(F32) + heard[2, 1, at, :].astype(F32))
            y_send[at, :] = far.astype(BF16)

        each(half // BLOCK, add)
        y_reduce(h).start()

    def add_heard(index):
        d, nf = chunk(index)
        h = jnp.where(d == 1, 0, 1)
        z_arrival(2, nf, h)

        def add(i):
            at = span(h * half + i * BLOCK, BLOCK)
            part[d, nf, at, :] = (part[d, nf, at, :].astype(F32) + heard[1, nf, at, :].astype(F32)).astype(BF16)

        each(half // BLOCK, add)
        z_copy(d, nf, h).start()

    @pl.when(moves)
    def _():
        def move(i):
            d = pick(i, (2, 1, 3, 0))
            arrival(stage.at[d], t_recv.at[d]).wait_recv()
            swap_copy(d).start()

        each(4, move)

    enter(0)
    relay(0)
    enter(1)
    enter(2)

    def half_chunk(t):
        i, first = t // 2, t % 2 == 0
        d, nf = chunk(i)
        h = jnp.where(d == 3, t % 2, 1 - t % 2)

        @pl.when(jnp.logical_and(first, i < 7))
        def _():
            relay(i + 1)

        @pl.when(t == 2 * Y_AT)
        def _():
            each(2, send_far)

        @pl.when(first)
        def _():
            complete(d, nf)

        @pl.when(t == 0)
        def _():
            loads[3].wait()
            swap.wait_recv()

        e = lane(nf)

        def product(j):
            at = span(h * half + j * STEP, STEP)
            acc = jnp.dot(tile[0, at, :], mirrored[d, e, 0:half, :], preferred_element_type=F32)
            acc += jnp.dot(tile[1, at, :], mirrored[d, e, half:, :], preferred_element_type=F32)
            part[d, nf, at, :] = acc.astype(BF16)

        each(half // STEP, product)

        @pl.when(jnp.logical_or(d == 2, jnp.logical_and(first, d != 0)))
        def _():
            z_copy(d, nf, h).start()

        @pl.when(jnp.logical_and(first, i < 5))
        def _():
            enter(i + 3)

        added = pick(i, [ADDED.get(k, -1) for k in range(8)])

        @pl.when(jnp.logical_and(jnp.logical_not(first), added >= 0))
        def _():
            add_heard(added)

    each(16, half_chunk)

    total = None
    for h in (1, 0):
        arrival(y_recv.at[span(h * half, half)], yr_recv.at[h]).wait_recv()
        z_arrival(1, 0, h)
        z_arrival(3, 0, h)

        def finish(b):
            at = span((b + h * (blocks // 2)) * BLOCK, BLOCK)
            value = part[0, 0, at, :].astype(F32) + y_recv[at, :].astype(F32)
            value = (value + (heard[0, 0, at, :].astype(F32) + heard[2, 0, at, :].astype(F32))).T
            mask = listed[col, row * blocks + b + h * (blocks // 2)].astype(F32)
            out[:, at] = -(value * mask)
            high = value.astype(BF16)
            split[0:BLOCK, at] = high
            split[BLOCK:, at] = (value - high.astype(F32)).astype(BF16)

        each(blocks // 2, finish)
        both = jnp.dot(split[:, h * half:(h + 1) * half], lhat[h * half:(h + 1) * half, :], preferred_element_type=F32)
        both = both[0:BLOCK] + both[BLOCK:]
        total = both if total is None else total + both

    d_send[...] = total.astype(BF16)

    def d_copy(step):
        to = (row + step + 1) % 8
        return remote(d_send, d_recv.at[row], dg_send.at[step], dg_recv.at[step], (to, col))

    each(7, lambda step: d_copy(step).start())
    d_recv[row] = d_send[...]
    each(7, lambda step: arrival(d_recv.at[(row + 7 - step) % 8], dg_recv.at[step]).wait_recv())
    total = d_recv[0].astype(F32)
    for other in range(1, 8):
        total = total + d_recv[other].astype(F32)
    loads[4].wait()
    diag_out[0] = pivot[0] + total

    swap.wait_send()
    for straight, when in ((True, stays), (False, moves)):

        @pl.when(when)
        def _():
            def sent(q):
                @pl.when(jnp.logical_or(q != x, x != z))
                def _():
                    t_copy(q, straight)[0].wait_send()

            each(4, sent)

    @pl.when(twice)
    def _():
        each(4, lambda q: t_twice(q).wait_send())

    def sent(d):
        @pl.when(moves)
        def _():
            swap_copy(d).wait_send()

        @pl.when(y_sends(d))
        def _():
            y_copy(d).wait_send()

        def sides(j):
            nf, side = j // 2, j % 2
            x_copy(d, nf, side).wait_send()
            f_copy(d, nf, side).wait_send()

            @pl.when(d != 0)
            def _():
                z_copy(d, nf, side).wait_send()

        each(4, sides)

    each(4, sent)
    each(2, lambda h: y_reduce(h).wait_send())
    each(7, lambda step: d_copy(step).wait_send())


def per_device(l_panel, inverse_tile, unit_inverse, pivot_inverse, listed):
    rows, width = l_panel.shape
    columns = inverse_tile.shape[1]
    dma = pltpu.SemaphoreType.DMA
    vmem = pl.BlockSpec(memory_space=pltpu.VMEM)
    hbm = pl.BlockSpec(memory_space=pltpu.HBM)
    operands = (listed, l_panel, inverse_tile, unit_inverse, pivot_inverse)
    return pl.pallas_call(
        kernel,
        out_shape=(
            jax.ShapeDtypeStruct((width, rows), F32),
            jax.ShapeDtypeStruct((1, width, width), F32),
        ),
        in_specs=[hbm] * 5,
        out_specs=(vmem, vmem),
        scratch_shapes=[
            pltpu.SMEM(listed.shape, jnp.int32),
            pltpu.VMEM((1, width, width), BF16),
            pltpu.VMEM((1, width, width), F32),
            pltpu.VMEM((rows, width), BF16),
            pltpu.VMEM((rows, width), BF16),
            pltpu.VMEM((2, rows, columns), BF16),
            pltpu.VMEM((4, 2, rows, width), BF16),
            pltpu.VMEM((4, 2, rows, width), BF16),
            pltpu.VMEM((3, 2, rows, width), BF16),
            pltpu.VMEM((rows, width), BF16),
            pltpu.VMEM((rows, width), BF16),
            pltpu.VMEM((4, rows // 4, width), BF16),
            pltpu.VMEM((2 * width, rows), BF16),
            pltpu.VMEM((width, width), BF16),
            pltpu.VMEM((8, width, width), BF16),
            dma((5,)),
            dma((2,)),
            dma((4,)),
            dma((4,)),
            dma((4,)),
            dma((4, 2)),
            dma((4,)),
            dma((4,)),
            dma((4, 2, 2)),
            dma((4, 2, 2)),
            dma((4, 2, 2)),
            dma((4, 2, 2)),
            dma((4, 2, 2)),
            dma((3, 2, 2)),
            dma((2,)),
            dma((2,)),
            dma((7,)),
            dma((7,)),
        ],
        compiler_params=pltpu.CompilerParams(
            collective_id=0, has_side_effects=True, vmem_limit_bytes=36 << 20
        ),
    )(*(pltpu.with_memory_space_constraint(a, pltpu.HBM) for a in operands))


def solution(mesh):
    return jax.shard_map(
        per_device,
        mesh=mesh,
        in_specs=(
            P("prow", "pcol"),
            P("prow", "pcol"),
            P("pcol", None, None),
            P("pcol", None, None),
            P(),
        ),
        out_specs=(P("pcol", "prow"), P("pcol", None, None)),
        check_vma=False,
    )
```

time: 440 us -> 93.9 us (0.21)
  waiting for transfers between devices: 364 us -> 0 us
  Pallas kernels: 0 us -> 91.6 us
  blocking collectives: 33.3 us -> 0 us
  matrix products: 17.7 us -> 0 us
  between operations: 13.8 us -> 0.64 us
  other arithmetic: 10.8 us -> 0 us
    psum x1 -> x0, waiting for transfers between devices: 182 us -> none  [broadcast(): return lax.psum(block, axis)]
    reduce_scatter x1 -> x0, waiting for transfers between devices: 102 us -> none  [per_device(): lax.psum_scatter(lax.dot_general(mirrored, inverse_tile, (((0,), (1,)), (...]
    pallas_call x0 -> x1, Pallas kernels: none -> 91.6 us  [per_device(): pl.pallas_call(kernel, out_shape=(jax.ShapeDtypeStruct((width, rows), F32...]
    all_gather x1 -> x0, waiting for transfers between devices: 80.2 us -> none  [per_device(): wide_rows = lax.all_gather(lhat_flat, 'pcol', axis=1, tiled=True)]
    psum x1 -> x0, blocking collectives: 33.3 us -> none  [per_device(): lax.psum(partial_diag.astype(jnp.bfloat16), 'prow').astype(jnp.float32)]
    dot_general x3 -> x0, matrix products: 17.7 us -> none  [the longest x1 14 us: per_device(): lax.dot_general(mirrored, inverse_tile, (((0,), (1,)), ((), ())), preferr...]
    select_n x1 -> x0, other arithmetic: 7.14 us -> none  [broadcast(): jnp.where(lax.axis_index(axis) == source, block, jnp.zeros_like(block))]
  transfers between devices with their start and end apart: 3 -> 0, of which waited for: 3 -> 0; matrix products, arithmetic and copies ran while one was open for 0% -> 0% of each run, Pallas kernels for 0% -> 0%
where the time goes in v3:
time: 93.9 us; the launch traced here: 93.8 us
  Pallas kernels  91.6 us (98%)
  local copies, waits for them, and re-layouts  1.6 us (2%)
    pallas_call x1, Pallas kernels, per_device(): pl.pallas_call(kernel, out_shape=(jax.ShapeDtypeStruct((width, rows), F32...  91.6 us

profile of v3, /device:TPU:0, one launch (start us, length us, event | category | flops | bytes accessed | tf_op | source)
XLA Modules:
  0.0 93.8 jit_solution(14259079303843299589)
XLA Ops:
  0.6 91.6 %shard_map.68 = (f32[128,2048]{1,0:T(8,128)S(1)}, f32[1,128,128]{2,1,0:T(8,128)S(1)}) custom-call(s32[16,128]{1,0:T(8,128)} %listed_hbm.1, bf16[2048,128]{1,0:T(8,128)(2,1)} %panel_hbm.1, bf16[2048,1024]{1,0:T(8,128)(2,1)} %tile_hbm.1, bf16[1,128,128]{2,1,0:T(8,128)(2,1)} %unit_hbm.1, f32[1,128,128]{2,1,0:T(8,128)} %pivot_hbm.1), custom_call_target="tpu_custom_call" | custom-call | tf_op jit(solution)/shard_map/pallas_call | solution.py:399
  92.2 1.0 %copy.9 = f32[128,2048]{1,0:T(8,128)} copy(f32[128,2048]{1,0:T(8,128)S(1)} %get-tuple-element.4) | data formatting | bytes 2097152
  93.2 0.6 copy.10

commit v4 on v3

--- a/solution.py
+++ b/solution.py
@@ -7,10 +7,14 @@
 
 MESH = pl.DeviceIdType.MESH
 BLOCK = 128
-STEP = 512
-ORDER = ((2, 0), (2, 1), (1, 1), (3, 1), (0, 1), (1, 0), (3, 0), (0, 0))
-ADDED = {3: 2, 4: 3, 5: 5, 6: 6}
+STEP = 1024
+ORDER = (
+    ((2, 0), (2, 1), (1, 1), (3, 1), (0, 0), (0, 1), (1, 0), (3, 0)),
+    ((2, 1), (2, 0), (1, 1), (3, 1), (0, 1), (0, 0), (1, 0), (3, 0)),
+)
+ADDED = ({7: 2, 9: 3, 13: 6, 14: 7}, {7: 2, 9: 3, 13: 6, 14: 7})
 Y_AT = 7
+AHEAD = 4
 F32 = jnp.float32
 BF16 = jnp.bfloat16
 
@@ -26,16 +30,12 @@
     return value
 
 
-def chunk(index):
-    return pick(index, [d for d, _ in ORDER]), pick(index, [nf for _, nf in ORDER])
-
-
 def kernel(
     listed_hbm, panel_hbm, tile_hbm, unit_hbm, pivot_hbm, out, diag_out,
     listed, unit, pivot, panel, lhat, tile, mirrored, part, heard, y_send, y_recv,
     stage, split, d_send, d_recv,
-    local_sem, core_sem, t_send, td_send, t_recv, in_recv, sw_send, ye_send,
-    x_send, x_recv, f_send, f_recv, z_send, z_recv, yr_send, yr_recv, dg_send, dg_recv,
+    local_sem, core_sem, t_send, t_recv, in_recv, sw_send, ye_send,
+    x_send, x_recv, f_send, f_recv, z_send, z_recv, p_send, p_recv, yr_send, yr_recv, dg_send, dg_recv,
 ):
     row, col = lax.axis_index("prow"), lax.axis_index("pcol")
     x, y_lo = row % 4, row // 4
@@ -45,6 +45,13 @@
     y_other = 2 * y_hi + 1 - y_lo
     stays = y_lo == y_hi
     moves = y_lo != y_hi
+
+    def choose(index, tables):
+        return jnp.where(stays, pick(index, tables[0]), pick(index, tables[1]))
+
+    def chunk(index):
+        return tuple(choose(index, [[c[k] for c in order] for order in ORDER]) for k in range(2))
+
     rows = panel.shape[0]
     half, quarter, eighth = rows // 2, rows // 4, rows // 8
     blocks = rows // BLOCK
@@ -96,8 +103,6 @@
     def greet_group(q):
         greet(device(q, y, x, core))
         greet(device(z, y, q, core))
-        greet(device(q, y_other, x, core))
-        greet(device(z, y_other, q, core))
 
     each(4, greet_group)
 
@@ -111,10 +116,9 @@
         lhat[at, :] = jnp.dot(masked, unit[0], preferred_element_type=F32).astype(BF16)
 
     each(blocks, lhat_block)
-    pl.semaphore_wait(barrier, 28)
+    pl.semaphore_wait(barrier, 20)
 
     d_mine = (x + 4 - z) % 4
-    twice = jnp.logical_and(stays, d_mine == 2)
 
     def t_copy(q, straight):
         at = span(q * quarter, quarter)
@@ -124,11 +128,6 @@
             dst, sem = stage.at[d_mine], t_recv.at[d_mine]
         return remote(lhat.at[at], dst, t_send.at[q], sem, device(q, y, x, core)), (lhat.at[at], dst, sem)
 
-    def t_twice(q):
-        at = span(q * quarter, quarter)
-        to = device(q, y_other, x, core)
-        return remote(lhat.at[at], mirrored.at[2, y_hi, at], td_send.at[q], in_recv.at[2, y_hi], to)
-
     for straight, when in ((True, stays), (False, moves)):
 
         @pl.when(when)
@@ -145,10 +144,6 @@
 
             each(4, send)
 
-    @pl.when(twice)
-    def _():
-        each(4, lambda q: t_twice(q).start())
-
     swap = remote(tile_hbm, tile.at[core], core_sem.at[0], core_sem.at[1], other_core)
     swap.start()
 
@@ -187,30 +182,64 @@
     def arrival(ref, sem):
         return remote(ref, ref, core_sem.at[0], sem, y_far)
 
-    def y_sends(d):
-        return jnp.logical_not(jnp.logical_and(stays, d == 2))
+    def wide(d, nf):
+        return jnp.logical_and(d == 0, jnp.logical_xor(stays, nf == 0))
+
+    def narrow(d, nf):
+        return jnp.logical_not(wide(d, nf))
+
+    def pass_copy(j):
+        q = pick(j, (from_x(0), from_x(1), (x + 2) % 4))
+        ref = quarter_of(0, y_lo, q)
+        return remote(ref, ref, p_send.at[j], p_recv.at[j], y_pair)
 
     def enter(index):
         d, nf = chunk(index)
         e = lane(nf)
-        arrival(quarter_of(d, e, x), in_recv.at[d, e]).wait_recv()
-
-        @pl.when(jnp.logical_and(y_lo == e, y_sends(d)))
+
+        @pl.when(jnp.logical_and(narrow(d, nf), jnp.logical_or(moves, nf == 1)))
+        def _():
+            arrival(quarter_of(d, e, x), in_recv.at[d, e]).wait_recv()
+
+        @pl.when(jnp.logical_and(moves, nf == 1))
         def _():
             y_copy(d).start()
 
-        for side in range(2):
-            x_copy(d, nf, side).start()
+        @pl.when(narrow(d, nf))
+        def _():
+            for side in range(2):
+                x_copy(d, nf, side).start()
 
     def relay(index):
         d, nf = chunk(index)
-        for side in range(2):
-            arrival(quarter_of(d, lane(nf), from_x(side)), x_recv.at[d, nf, side]).wait_recv()
-            f_copy(d, nf, side).start()
+
+        @pl.when(narrow(d, nf))
+        def _():
+            for side in range(2):
+                arrival(quarter_of(d, lane(nf), from_x(side)), x_recv.at[d, nf, side]).wait_recv()
+                f_copy(d, nf, side).start()
+
+                @pl.when(d == 0)
+                def _():
+                    pass_copy(side).start()
 
     def complete(d, nf):
-        for side in range(2):
-            arrival(eighth_of(d, lane(nf), (x + 2) % 4, side), f_recv.at[d, nf, side]).wait_recv()
+        e = lane(nf)
+
+        @pl.when(narrow(d, nf))
+        def _():
+            for side in range(2):
+                arrival(eighth_of(d, e, (x + 2) % 4, side), f_recv.at[d, nf, side]).wait_recv()
+
+            @pl.when(d == 0)
+            def _():
+                pass_copy(2).start()
+
+        @pl.when(wide(d, nf))
+        def _():
+            arrival(quarter_of(0, e, x), in_recv.at[0, e]).wait_recv()
+            for j, q in enumerate((from_x(0), from_x(1), (x + 2) % 4)):
+                arrival(quarter_of(0, e, q), p_recv.at[j]).wait_recv()
 
     def z_copy(d, nf, h):
         at = span(h * half, half)
@@ -259,15 +288,24 @@
 
         each(4, move)
 
+    @pl.when(stays)
+    def _():
+        def pass_on(i):
+            d = pick(i, (2, 1, 3, 0))
+            arrival(quarter_of(d, y_hi, x), in_recv.at[d, y_hi]).wait_recv()
+            y_copy(d).start()
+
+        each(4, pass_on)
+
     enter(0)
     relay(0)
-    enter(1)
-    enter(2)
+    for index in range(1, AHEAD):
+        enter(index)
 
     def half_chunk(t):
         i, first = t // 2, t % 2 == 0
         d, nf = chunk(i)
-        h = jnp.where(d == 3, t % 2, 1 - t % 2)
+        h = jnp.where(jnp.logical_and(d == 3, nf == 1), t % 2, 1 - t % 2)
 
         @pl.when(jnp.logical_and(first, i < 7))
         def _():
@@ -276,6 +314,10 @@
         @pl.when(t == 2 * Y_AT)
         def _():
             each(2, send_far)
+
+        @pl.when(jnp.logical_and(first, i < 8 - AHEAD))
+        def _():
+            enter(i + AHEAD)
 
         @pl.when(first)
         def _():
@@ -296,21 +338,19 @@
 
         each(half // STEP, product)
 
-        @pl.when(jnp.logical_or(d == 2, jnp.logical_and(first, d != 0)))
+        @pl.when(jnp.logical_or(d == 2, d == jnp.where(h == 1, 1, 3)))
         def _():
             z_copy(d, nf, h).start()
 
-        @pl.when(jnp.logical_and(first, i < 5))
-        def _():
-            enter(i + 3)
-
-        added = pick(i, [ADDED.get(k, -1) for k in range(8)])
-
-        @pl.when(jnp.logical_and(jnp.logical_not(first), added >= 0))
+        added = choose(t, [[table.get(k, -1) for k in range(16)] for table in ADDED])
+
+        @pl.when(added >= 0)
         def _():
             add_heard(added)
 
     each(16, half_chunk)
+    if Y_AT == 8:
+        each(2, send_far)
 
     total = None
     for h in (1, 0):
@@ -360,23 +400,20 @@
 
             each(4, sent)
 
-    @pl.when(twice)
-    def _():
-        each(4, lambda q: t_twice(q).wait_send())
-
     def sent(d):
         @pl.when(moves)
         def _():
             swap_copy(d).wait_send()
 
-        @pl.when(y_sends(d))
-        def _():
-            y_copy(d).wait_send()
+        y_copy(d).wait_send()
 
         def sides(j):
             nf, side = j // 2, j % 2
-            x_copy(d, nf, side).wait_send()
-            f_copy(d, nf, side).wait_send()
+
+            @pl.when(narrow(d, nf))
+            def _():
+                x_copy(d, nf, side).wait_send()
+                f_copy(d, nf, side).wait_send()
 
             @pl.when(d != 0)
             def _():
@@ -385,6 +422,7 @@
         each(4, sides)
 
     each(4, sent)
+    each(3, lambda j: pass_copy(j).wait_send())
     each(2, lambda h: y_reduce(h).wait_send())
     each(7, lambda step: d_copy(step).wait_send())
 
@@ -424,7 +462,6 @@
             dma((2,)),
             dma((4,)),
             dma((4,)),
-            dma((4,)),
             dma((4, 2)),
             dma((4,)),
             dma((4,)),
@@ -434,6 +471,8 @@
             dma((4, 2, 2)),
             dma((4, 2, 2)),
             dma((3, 2, 2)),
+            dma((3,)),
+            dma((3,)),
             dma((2,)),
             dma((2,)),
             dma((7,)),

time: 93.9 us -> 83.8 us (0.89)
  Pallas kernels: 91.6 us -> 81.5 us
    pallas_call x1, Pallas kernels: 91.6 us -> 81.5 us  [per_device(): pl.pallas_call(kernel, out_shape=(jax.ShapeDtypeStruct((width, rows), F32...]
where the time goes in v4:
time: 83.8 us; the launch traced here: 83.7 us
  Pallas kernels  81.5 us (97%)
  local copies, waits for them, and re-layouts  1.6 us (2%)
    pallas_call x1, Pallas kernels, per_device(): pl.pallas_call(kernel, out_shape=(jax.ShapeDtypeStruct((width, rows), F32...  81.5 us

profile of v4, /device:TPU:0, one launch (start us, length us, event | category | flops | bytes accessed | tf_op | source)
XLA Modules:
  0.0 83.7 jit_solution(5968629489078206527)
XLA Ops:
  0.6 81.5 %shard_map.68 = (f32[128,2048]{1,0:T(8,128)S(1)}, f32[1,128,128]{2,1,0:T(8,128)S(1)}) custom-call(s32[16,128]{1,0:T(8,128)} %listed_hbm.1, bf16[2048,128]{1,0:T(8,128)(2,1)} %panel_hbm.1, bf16[2048,1024]{1,0:T(8,128)(2,1)} %tile_hbm.1, bf16[1,128,128]{2,1,0:T(8,128)(2,1)} %unit_hbm.1, f32[1,128,128]{2,1,0:T(8,128)} %pivot_hbm.1), custom_call_target="tpu_custom_call" | custom-call | tf_op jit(solution)/shard_map/pallas_call | solution.py:437
  82.1 1.0 %copy.9 = f32[128,2048]{1,0:T(8,128)} copy(f32[128,2048]{1,0:T(8,128)S(1)} %get-tuple-element.4) | data formatting | bytes 2097152
  83.1 0.6 copy.10

commit v5 on v4

--- a/solution.py
+++ b/solution.py
@@ -260,11 +260,11 @@
         z_arrival(3, 1, h)
 
         def add(i):
-            at = span(h * half + i * BLOCK, BLOCK)
+            at = span(h * half + i * 2 * BLOCK, 2 * BLOCK)
             far = part[0, 1, at, :].astype(F32) + (heard[0, 1, at, :].astype(F32) + heard[2, 1, at, :].astype(F32))
             y_send[at, :] = far.astype(BF16)
 
-        each(half // BLOCK, add)
+        each(half // (2 * BLOCK), add)
         y_reduce(h).start()
 
     def add_heard(index):
@@ -273,10 +273,10 @@
         z_arrival(2, nf, h)
 
         def add(i):
-            at = span(h * half + i * BLOCK, BLOCK)
+            at = span(h * half + i * 2 * BLOCK, 2 * BLOCK)
             part[d, nf, at, :] = (part[d, nf, at, :].astype(F32) + heard[1, nf, at, :].astype(F32)).astype(BF16)
 
-        each(half // BLOCK, add)
+        each(half // (2 * BLOCK), add)
         z_copy(d, nf, h).start()
 
     @pl.when(moves)
@@ -358,17 +358,19 @@
         z_arrival(1, 0, h)
         z_arrival(3, 0, h)
 
-        def finish(b):
-            at = span((b + h * (blocks // 2)) * BLOCK, BLOCK)
-            value = part[0, 0, at, :].astype(F32) + y_recv[at, :].astype(F32)
-            value = (value + (heard[0, 0, at, :].astype(F32) + heard[2, 0, at, :].astype(F32))).T
-            mask = listed[col, row * blocks + b + h * (blocks // 2)].astype(F32)
-            out[:, at] = -(value * mask)
-            high = value.astype(BF16)
-            split[0:BLOCK, at] = high
-            split[BLOCK:, at] = (value - high.astype(F32)).astype(BF16)
-
-        each(blocks // 2, finish)
+        def finish(group):
+            for step in range(4):
+                b = 4 * group + step + h * (blocks // 2)
+                at = span(b * BLOCK, BLOCK)
+                value = part[0, 0, at, :].astype(F32) + y_recv[at, :].astype(F32)
+                value = (value + (heard[0, 0, at, :].astype(F32) + heard[2, 0, at, :].astype(F32))).T
+                mask = listed[col, row * blocks + b].astype(F32)
+                out[:, at] = -(value * mask)
+                high = value.astype(BF16)
+                split[0:BLOCK, at] = high
+                split[BLOCK:, at] = (value - high.astype(F32)).astype(BF16)
+
+        each(blocks // 8, finish)
         both = jnp.dot(split[:, h * half:(h + 1) * half], lhat[h * half:(h + 1) * half, :], preferred_element_type=F32)
         both = both[0:BLOCK] + both[BLOCK:]
         total = both if total is None else total + both
@@ -381,6 +383,42 @@
 
     each(7, lambda step: d_copy(step).start())
     d_recv[row] = d_send[...]
+    swap.wait_send()
+    for straight, when in ((True, stays), (False, moves)):
+
+        @pl.when(when)
+        def _():
+            def sent(q):
+                @pl.when(jnp.logical_or(q != x, x != z))
+                def _():
+                    t_copy(q, straight)[0].wait_send()
+
+            each(4, sent)
+
+    def sent(d):
+        @pl.when(moves)
+        def _():
+            swap_copy(d).wait_send()
+
+        y_copy(d).wait_send()
+
+        def sides(j):
+            nf, side = j // 2, j % 2
+
+            @pl.when(narrow(d, nf))
+            def _():
+                x_copy(d, nf, side).wait_send()
+                f_copy(d, nf, side).wait_send()
+
+            @pl.when(d != 0)
+            def _():
+                z_copy(d, nf, side).wait_send()
+
+        each(4, sides)
+
+    each(4, sent)
+    each(3, lambda j: pass_copy(j).wait_send())
+    each(2, lambda h: y_reduce(h).wait_send())
     each(7, lambda step: arrival(d_recv.at[(row + 7 - step) % 8], dg_recv.at[step]).wait_recv())
     total = d_recv[0].astype(F32)
     for other in range(1, 8):
@@ -388,42 +426,6 @@
     loads[4].wait()
     diag_out[0] = pivot[0] + total
 
-    swap.wait_send()
-    for straight, when in ((True, stays), (False, moves)):
-
-        @pl.when(when)
-        def _():
-            def sent(q):
-                @pl.when(jnp.logical_or(q != x, x != z))
-                def _():
-                    t_copy(q, straight)[0].wait_send()
-
-            each(4, sent)
-
-    def sent(d):
-        @pl.when(moves)
-        def _():
-            swap_copy(d).wait_send()
-
-        y_copy(d).wait_send()
-
-        def sides(j):
-            nf, side = j // 2, j % 2
-
-            @pl.when(narrow(d, nf))
-            def _():
-                x_copy(d, nf, side).wait_send()
-                f_copy(d, nf, side).wait_send()
-
-            @pl.when(d != 0)
-            def _():
-                z_copy(d, nf, side).wait_send()
-
-        each(4, sides)
-
-    each(4, sent)
-    each(3, lambda j: pass_copy(j).wait_send())
-    each(2, lambda h: y_reduce(h).wait_send())
     each(7, lambda step: d_copy(step).wait_send())
 
 

time: 83.8 us -> 82.8 us (0.988)
  Pallas kernels: 81.5 us -> 80.5 us
    pallas_call x1, Pallas kernels: 81.5 us -> 80.5 us  [per_device(): pl.pallas_call(kernel, out_shape=(jax.ShapeDtypeStruct((width, rows), F32...]
where the time goes in v5:
time: 82.8 us; the launch traced here: 82.7 us
  Pallas kernels  80.5 us (97%)
  local copies, waits for them, and re-layouts  1.6 us (2%)
    pallas_call x1, Pallas kernels, per_device(): pl.pallas_call(kernel, out_shape=(jax.ShapeDtypeStruct((width, rows), F32...  80.5 us

profile of v5, /device:TPU:0, one launch (start us, length us, event | category | flops | bytes accessed | tf_op | source)
XLA Modules:
  0.0 82.7 jit_solution(17834493401343660262)
XLA Ops:
  0.6 80.5 %shard_map.68 = (f32[128,2048]{1,0:T(8,128)S(1)}, f32[1,128,128]{2,1,0:T(8,128)S(1)}) custom-call(s32[16,128]{1,0:T(8,128)} %listed_hbm.1, bf16[2048,128]{1,0:T(8,128)(2,1)} %panel_hbm.1, bf16[2048,1024]{1,0:T(8,128)(2,1)} %tile_hbm.1, bf16[1,128,128]{2,1,0:T(8,128)(2,1)} %unit_hbm.1, f32[1,128,128]{2,1,0:T(8,128)} %pivot_hbm.1), custom_call_target="tpu_custom_call" | custom-call | tf_op jit(solution)/shard_map/pallas_call | solution.py:439
  81.1 1.0 %copy.9 = f32[128,2048]{1,0:T(8,128)} copy(f32[128,2048]{1,0:T(8,128)S(1)} %get-tuple-element.4) | data formatting | bytes 2097152
  82.1 0.6 copy.10

commit v6 on v5

--- a/solution.py
+++ b/solution.py
@@ -109,13 +109,15 @@
     for load in loads[:3]:
         load.wait()
 
-    def lhat_block(b):
-        at = span(b * BLOCK, BLOCK)
-        mask = listed[col, row * blocks + b].astype(F32)
-        masked = (panel[at, :].astype(F32) * mask).astype(BF16)
-        lhat[at, :] = jnp.dot(masked, unit[0], preferred_element_type=F32).astype(BF16)
-
-    each(blocks, lhat_block)
+    def lhat_quarter(q):
+        parts = []
+        for b in range(quarter // BLOCK):
+            mask = listed[col, row * blocks + q * (quarter // BLOCK) + b].astype(F32)
+            parts.append((panel[span(q * quarter + b * BLOCK, BLOCK), :].astype(F32) * mask).astype(BF16))
+        normalized = jnp.dot(jnp.concatenate(parts, axis=0), unit[0], preferred_element_type=F32)
+        lhat[span(q * quarter, quarter), :] = normalized.astype(BF16)
+
+    each(4, lhat_quarter)
     pl.semaphore_wait(barrier, 20)
 
     d_mine = (x + 4 - z) % 4

time: 82.8 us -> 82.9 us (level)
  no operation moved by 1% of the time
where the time goes in v6:
time: 82.9 us; the launch traced here: 82.8 us
  Pallas kernels  80.6 us (97%)
  local copies, waits for them, and re-layouts  1.6 us (2%)
    pallas_call x1, Pallas kernels, per_device(): pl.pallas_call(kernel, out_shape=(jax.ShapeDtypeStruct((width, rows), F32...  80.6 us

profile of v6, /device:TPU:0, one launch (start us, length us, event | category | flops | bytes accessed | tf_op | source)
XLA Modules:
  0.0 82.8 jit_solution(10286229066977023066)
XLA Ops:
  0.6 80.6 %shard_map.68 = (f32[128,2048]{1,0:T(8,128)S(1)}, f32[1,128,128]{2,1,0:T(8,128)S(1)}) custom-call(s32[16,128]{1,0:T(8,128)} %listed_hbm.1, bf16[2048,128]{1,0:T(8,128)(2,1)} %panel_hbm.1, bf16[2048,1024]{1,0:T(8,128)(2,1)} %tile_hbm.1, bf16[1,128,128]{2,1,0:T(8,128)(2,1)} %unit_hbm.1, f32[1,128,128]{2,1,0:T(8,128)} %pivot_hbm.1), custom_call_target="tpu_custom_call" | custom-call | tf_op jit(solution)/shard_map/pallas_call | solution.py:441
  81.2 1.0 %copy.9 = f32[128,2048]{1,0:T(8,128)} copy(f32[128,2048]{1,0:T(8,128)S(1)} %get-tuple-element.4) | data formatting | bytes 2097152
  82.2 0.6 copy.10
